TPU v7x, 256 devices: a whole 4x4x8 slice. The times are simulated.
256 devices in a mesh: row: 8 (over x, core), col: 32 (over z, y).
Axes of the slice: x: 4, y: 4, z: 8, core: 2. Of those that a mesh axis runs over, the one named last changes fastest.
Arguments:
- density: bfloat16 [256, 16, 128, 128], P(('row', 'col')), as said below
- cols: int32 [256, 16], replicated, may hold values from 0 to 255, as said below
Outputs:
- new_density: float32 [256, 16, 128, 128], P(('row', 'col'))
Inputs may be any that keep to these rules, and one draw needn't show every extreme that they name: Block row b is held by the device with row index (b) // 32 and col index q = (b) % 32. cols[b, 0] = b and a row's entries are distinct. For 1 <= t <= 7, cols[b, 2t - 1] is held by a device of col index q + t and cols[b, 2t] by one of col index q - t (modulo 32); cols[b, 15] by one of col index q + 16. The pattern is symmetric with mirrored slots: if j = cols[b, s] then cols[j, s'] = b, where s' = s for s = 0 and s = 15, s' = s + 1 for odd s below 15, and s' = s - 1 for even s above 0. density[b, s] is exactly the transpose of density[cols[b, s], s'], with s' the mirrored slot.
All inputs are finite; a program needn't handle non-finite values.
Results may differ from a plain program's by a relative error of at most 0.0093.
Values may be sent and summed in bfloat16 or wider, within the bound.
No kernel may reach another device: no remote copies, remote signals or barrier semaphores. Data moves between devices by JAX's collectives and lax.ppermute only.
A program may use at most 128 MiB of HBM per device.

v0:
```python
import jax
import jax.numpy as jnp
from jax import lax
from jax.sharding import PartitionSpec as P


def shifted(value, axis, by):
    length = lax.axis_size(axis)
    return lax.ppermute(value, axis, [(i, (i + by) % length) for i in range(length)])


def slot_offsets(slot_count, grid_cols):
    offsets = [0]
    for stride in range(1, (slot_count - 2) // 2 + 1):
        offsets = offsets + [stride, -stride]
    return offsets + [grid_cols // 2]


def mirror_slots(slot_count):
    order = [0]
    for stride in range(1, (slot_count - 2) // 2 + 1):
        order = order + [2 * stride, 2 * stride - 1]
    return order + [slot_count - 1]


def per_device(density, cols):
    rows_here = density.shape[0]
    slot_count = density.shape[1]
    grid_cols = lax.axis_size("col")
    my_row = lax.axis_index("row")
    my_col = lax.axis_index("col")
    offsets = slot_offsets(slot_count, grid_cols)
    mirror = jnp.array(mirror_slots(slot_count), jnp.int32)
    shift_ids = jnp.array(offsets, jnp.int32)
    local_ids = jnp.arange(rows_here, dtype=jnp.int32)
    slot_ids = jnp.arange(slot_count, dtype=jnp.int32)
    source_col = (my_col - shift_ids) % grid_cols
    tile_rows = (my_row * grid_cols + source_col)[:, None] * rows_here + local_ids[None, :]
    left_cols = cols[tile_rows]
    targets = left_cols[slot_ids[:, None], local_ids[None, :], slot_ids[:, None]]
    target_cols = cols[targets]
    matches = left_cols[..., :, None] == target_cols[..., None, :]
    present = jnp.any(matches, axis=-1)
    found_slot = jnp.sum(jnp.where(matches, slot_ids, 0), axis=-1)
    target_rank = targets // rows_here // grid_cols * rows_here + targets % rows_here
    present_mask = present[..., None, None]
    gathered = lax.all_gather(density, "col", axis=0, tiled=True)
    left_blocks = gathered[source_col[:, None] * rows_here + local_ids[None, :]]
    column_blocks = lax.all_gather(density, "row", axis=0, tiled=True)
    right_blocks = column_blocks[target_rank[:, :, None], found_slot]
    right_blocks = jnp.where(present_mask, right_blocks, jnp.zeros((), right_blocks.dtype))
    square_tile = jnp.einsum(
        "sltab,sltcb->slac", left_blocks, right_blocks, preferred_element_type=jnp.float32
    )
    square_half = square_tile.astype(jnp.bfloat16)
    square_panel = lax.all_gather(square_half[None], "row", axis=0, tiled=True)
    inner_row = left_cols // rows_here // grid_cols
    inner_local = left_cols % rows_here
    from_square = square_panel[inner_row, mirror[found_slot], inner_local]
    from_square = jnp.where(present_mask, from_square, jnp.zeros((), from_square.dtype))
    cube_tile = jnp.einsum(
        "sltab,sltbc->slac", left_blocks, from_square, preferred_element_type=jnp.float32
    )
    new_tiles = 3.0 * square_tile - 2.0 * cube_tile
    returned_pieces = []
    for position, stride in enumerate(offsets):
        if stride == 0:
            returned_pieces.append(new_tiles[position])
        else:
            returned_pieces.append(shifted(new_tiles[position], "col", -stride))
    return jnp.stack(returned_pieces, axis=1)


def solution(mesh):
    in_specs = (P(("row", "col"), None, None, None), P())
    out_specs = P(("row", "col"), None, None, None)
    return jax.shard_map(
        per_device, mesh=mesh, in_specs=in_specs, out_specs=out_specs, check_vma=False
    )
```

profile of v0, /device:TPU:48, one launch (start us, length us, event | category | flops | bytes accessed | tf_op | source)
XLA Modules:
  0.0 314.3 jit_solution(2974334684125972960)
XLA Ops:
  6.5 0.0 all-gather.7.cloned.1.call-start
  6.5 0.7 all-gather.7.cloned.1.call-update
  7.3 0.0 all-gather.5.cloned.1.call-start
  7.3 0.7 all-gather.5.cloned.1.call-update
  8.0 0.0 all-gather.9.cloned.1.call-start
  8.1 0.8 copy.11
  8.9 0.7 compare_select_fusion.6
  9.6 0.6 gather_fusion.1
  10.2 0.7 gather_fusion.2
  10.9 0.6 gather_fusion.3
  11.4 0.4 fusion.20
  11.9 0.1 broadcast_in_dim.57
  12.0 0.1 reshape.430
  12.1 0.4 compare_reduce_fusion
  12.5 33.8 %all-gather.7.cloned.1.call-done = bf16[8,16,128,128]{3,2,1,0:T(8,128)(2,1)} async-done(((bf16[1,16,128,128]{3,2,1,0:T(8,128)(2,1)}), bf16[8,16,128,128]{3,2,1,0:T(8,128)(2,1)}) %all-gather.7.cloned.1.call-update) | async-done | bytes 4194320 | tf_op jit(solution)/shard_map/all_gather | solution.py:49
  46.3 12.1 %gather_fusion.4 = bf16[256,128,128]{2,1,0:T(8,128)(2,1)} fusion(bf16[8,16,128,128]{3,2,1,0:T(8,128)(2,1)} %all-gather.7.cloned.1.call-done, s32[256]{0:T(256)S(1)} %reshape.430), kind=kCustom, calls=%fused_computation.4 | custom fusion | bytes 16779264 | tf_op jit(solution)/shard_map/gather | solution.py:50
  58.4 127.8 %all-gather.5.cloned.1.call-done = bf16[32,16,128,128]{3,2,1,0:T(8,128)(2,1)} async-done(((bf16[1,16,128,128]{3,2,1,0:T(8,128)(2,1)}), bf16[32,16,128,128]{3,2,1,0:T(8,128)(2,1)}) %all-gather.5.cloned.1.call-update) | async-done | bytes 16777232 | tf_op jit(solution)/shard_map/all_gather | solution.py:47
  186.2 10.6 %gather_fusion = bf16[16,16,128,128]{3,2,1,0:T(8,128)(2,1)} fusion(bf16[32,16,128,128]{3,2,1,0:T(8,128)(2,1)} %all-gather.5.cloned.1.call-done, s32[1024]{0:T(1024)S(1)} %pad_clamp_fusion.3), kind=kCustom, calls=%fused_computation | custom fusion | bytes 16777280 | tf_op jit(solution)/shard_map/gather | solution.py:48
  196.8 0.0 copy-start
  196.8 9.0 %fusion.38 = (bf16[16,128,128]{2,1,0:T(8,128)(2,1)}, f32[16,128,128]{2,1,0:T(8,128)S(1)}) fusion(bf16[16,16,128,128]{3,2,1,0:T(8,128)(2,1)} %gather_fusion, bf16[16,16,128,128]{3,2,1,0:T(8,128)(2,1)} %bitcast.90, pred[16,16]{1,0:T(8,128)(4,1)S(1)} %compare_reduce_fusion), kind=kOutput, calls=%fused_computation.88 | convolution fusion | flops 1078198272 | bytes 18350336 | tf_op jit(solution)/shard_map/sltab,sltcb->slac/dot_general | solution.py:52
  205.8 0.0 all-gather.9.cloned.1.call-update
  205.8 0.1 reshape.438
  205.9 0.0 copy-done
  205.9 1.9 gather_fusion.5
  207.8 0.1 gather.43
  207.9 0.1 reshape.446
  208.0 33.0 %all-gather.9.cloned.1.call-done = bf16[128,128,128]{2,1,0:T(8,128)(2,1)} async-done(((bf16[16,128,128]{2,1,0:T(8,128)(2,1)}), bf16[128,128,128]{2,1,0:T(8,128)(2,1)}) %all-gather.9.cloned.1.call-update) | async-done | bytes 4194320 | tf_op jit(solution)/shard_map/all_gather | solution.py:56
  241.0 12.2 %gather_fusion.6 = bf16[256,128,128]{2,1,0:T(8,128)(2,1)} fusion(bf16[8,16,1,128,128]{4,3,1,0,2:T(8,128)(2,1)} %bitcast.89, s32[256]{0:T(256)S(1)} %reshape.446), kind=kCustom, calls=%fused_computation.6 | custom fusion | bytes 16780288 | tf_op jit(solution)/shard_map/gather | solution.py:59
  253.2 8.2 %fusion.17 = f32[16,128,128]{2,1,0:T(8,128)S(1)} fusion(bf16[16,16,128,128]{3,2,1,0:T(8,128)(2,1)} %gather_fusion, bf16[16,16,128,128]{3,2,1,0:T(8,128)(2,1)} %bitcast.91, pred[16,16]{1,0:T(8,128)(4,1)S(1)} %compare_reduce_fusion, f32[16,128,128]{2,1,0:T(8,128)S(1)} %get-tuple-element.23), kind=kOutput, calls=%fused_computation.18 | convolution fusion | flops 1078722560 | bytes 18874624 | tf_op jit(solution)/shard_map/sltab,sltbc->slac/dot_general | solution.py:61
  261.5 0.1 fusion.37
  261.5 0.8 collective-permute-start
  262.3 1.5 collective-permute-start.1
  263.8 1.2 collective-permute-start.2
  265.0 3.2 %collective-permute-start.3 = (f32[1,128,128]{2,1,0:T(8,128)S(1)}, f32[1,128,128]{2,1,0:T(8,128)S(1)}, u32[]{:S(2)}, u32[]{:S(2)}) collective-permute-start(f32[1,128,128]{2,1,0:T(8,128)S(1)} %get-tuple-element.18), channel_id=1, source_target_pairs={{0,2},{1,3},{2,4},{3,5},{4,6},{5,7},{6,8},{7,9},{8,10},{9,11},{10,... | collective-permute-start | bytes 196616 | tf_op jit(solution)/shard_map/ppermute | solution.py:9
  268.3 3.2 %collective-permute-start.4 = (f32[1,128,128]{2,1,0:T(8,128)S(1)}, f32[1,128,128]{2,1,0:T(8,128)S(1)}, u32[]{:S(2)}, u32[]{:S(2)}) collective-permute-start(f32[1,128,128]{2,1,0:T(8,128)S(1)} %get-tuple-element.17), channel_id=1, source_target_pairs={{0,29},{1,30},{2,31},{3,0},{4,1},{5,2},{6,3},{7,4},{8,5},{9,6},{10... | collective-permute-start | bytes 196616 | tf_op jit(solution)/shard_map/ppermute | solution.py:9
  271.4 0.0 collective-permute-done
  271.4 0.0 collective-permute-start.5
  271.4 0.0 collective-permute-done.1
  271.4 5.9 %collective-permute-start.6 = (f32[1,128,128]{2,1,0:T(8,128)S(1)}, f32[1,128,128]{2,1,0:T(8,128)S(1)}, u32[]{:S(2)}, u32[]{:S(2)}) collective-permute-start(f32[1,128,128]{2,1,0:T(8,128)S(1)} %get-tuple-element.15), channel_id=1, source_target_pairs={{0,28},{1,29},{2,30},{3,31},{4,0},{5,1},{6,2},{7,3},{8,4},{9,5},{1... | collective-permute-start | bytes 196616 | tf_op jit(solution)/shard_map/ppermute | solution.py:9
  277.3 0.0 collective-permute-done.2
  277.3 0.1 collective-permute-start.7
  277.4 0.0 collective-permute-done.3
  277.4 3.4 %collective-permute-start.8 = (f32[1,128,128]{2,1,0:T(8,128)S(1)}, f32[1,128,128]{2,1,0:T(8,128)S(1)}, u32[]{:S(2)}, u32[]{:S(2)}) collective-permute-start(f32[1,128,128]{2,1,0:T(8,128)S(1)} %get-tuple-element.13), channel_id=1, source_target_pairs={{0,27},{1,28},{2,29},{3,30},{4,31},{5,0},{6,1},{7,2},{8,3},{9,4},{... | collective-permute-start | bytes 196616 | tf_op jit(solution)/shard_map/ppermute | solution.py:9
  280.9 0.0 collective-permute-done.4
  280.9 0.2 collective-permute-start.9
  281.1 0.0 collective-permute-done.5
  281.1 3.7 %collective-permute-start.10 = (f32[1,128,128]{2,1,0:T(8,128)S(1)}, f32[1,128,128]{2,1,0:T(8,128)S(1)}, u32[]{:S(2)}, u32[]{:S(2)}) collective-permute-start(f32[1,128,128]{2,1,0:T(8,128)S(1)} %get-tuple-element.11), channel_id=1, source_target_pairs={{0,26},{1,27},{2,28},{3,29},{4,30},{5,31},{6,0},{7,1},{8,2},{9,3},... | collective-permute-start | bytes 196616 | tf_op jit(solution)/shard_map/ppermute | solution.py:9
  284.8 0.0 collective-permute-done.6
  284.8 1.7 collective-permute-start.11
  286.6 0.0 collective-permute-done.7
  286.6 10.8 %collective-permute-start.12 = (f32[1,128,128]{2,1,0:T(8,128)S(1)}, f32[1,128,128]{2,1,0:T(8,128)S(1)}, u32[]{:S(2)}, u32[]{:S(2)}) collective-permute-start(f32[1,128,128]{2,1,0:T(8,128)S(1)} %get-tuple-element.9), channel_id=1, source_target_pairs={{0,25},{1,26},{2,27},{3,28},{4,29},{5,30},{6,31},{7,0},{8,1},{9,2}... | collective-permute-start | bytes 196616 | tf_op jit(solution)/shard_map/ppermute | solution.py:9
  297.4 0.0 collective-permute-done.8
  297.4 0.1 collective-permute-start.13
  297.5 0.0 collective-permute-done.9
  297.6 3.0 collective-permute-start.14
  300.5 0.0 collective-permute-done.10
  300.5 0.0 collective-permute-done.11
  300.6 0.0 collective-permute-done.12
  300.6 5.5 %collective-permute-done.13 = f32[1,128,128]{2,1,0:T(8,128)S(1)} collective-permute-done((f32[1,128,128]{2,1,0:T(8,128)S(1)}, f32[1,128,128]{2,1,0:T(8,128)S(1)}, u32[]{:S(2)}, u32[]{:S(2)}) %collective-permute-start.13) | collective-permute-done | bytes 65568 | tf_op jit(solution)/shard_map/ppermute | solution.py:9
  306.1 0.0 copy-start.1
  306.1 0.0 collective-permute-done.14
  306.1 1.0 copy-done.1
  307.1 0.6 bitcast_dynamic-update-slice_fusion
  (33 shorter events, 0.2 us)
Async XLA Ops:
  6.5 39.8 %all-gather.7.cloned.1.call-start = ((), (), s32[]{:S(2)}) async-start(), calls=%async_computation.1 | async-start | bytes 4718592 | tf_op jit(solution)/shard_map/all_gather | solution.py:49
  7.3 179.0 %all-gather.5.cloned.1.call-start = ((), (), s32[]{:S(2)}) async-start(), calls=%async_computation | async-start | bytes 17301504 | tf_op jit(solution)/shard_map/all_gather | solution.py:47
  8.0 233.0 %all-gather.9.cloned.1.call-start = ((), (), s32[]{:S(2)}) async-start(), calls=%async_computation.2 | async-start | bytes 4718592 | tf_op jit(solution)/shard_map/all_gather | solution.py:56
  196.8 9.1 %copy-start = (s32[16]{0:T(128)S(1)}, s32[16]{0:T(128)}, u32[]{:S(2)}) copy-start(s32[16]{0:T(128)} %constant.115.clone) | copy-start | bytes 196
  261.5 9.9 %collective-permute-start = (f32[1,128,128]{2,1,0:T(8,128)S(1)}, f32[1,128,128]{2,1,0:T(8,128)S(1)}, u32[]{:S(2)}, u32[]{:S(2)}) collective-permute-start(f32[1,128,128]{2,1,0:T(8,128)S(1)} %get-tuple-element.21), channel_id=1, source_target_pairs={{0,31},{1,0},{2,1},{3,2},{4,3},{5,4},{6,5},{7,6},{8,7},{9,8},{10,9... | collective-permute-start | bytes 196616 | tf_op jit(solution)/shard_map/ppermute | solution.py:9
  262.3 9.1 %collective-permute-start.1 = (f32[1,128,128]{2,1,0:T(8,128)S(1)}, f32[1,128,128]{2,1,0:T(8,128)S(1)}, u32[]{:S(2)}, u32[]{:S(2)}) collective-permute-start(f32[1,128,128]{2,1,0:T(8,128)S(1)} %get-tuple-element.20), channel_id=1, source_target_pairs={{0,1},{1,2},{2,3},{3,4},{4,5},{5,6},{6,7},{7,8},{8,9},{9,10},{10,1... | collective-permute-start | bytes 196616 | tf_op jit(solution)/shard_map/ppermute | solution.py:9
  263.8 13.5 %collective-permute-start.2 = (f32[1,128,128]{2,1,0:T(8,128)S(1)}, f32[1,128,128]{2,1,0:T(8,128)S(1)}, u32[]{:S(2)}, u32[]{:S(2)}) collective-permute-start(f32[1,128,128]{2,1,0:T(8,128)S(1)} %get-tuple-element.19), channel_id=1, source_target_pairs={{0,30},{1,31},{2,0},{3,1},{4,2},{5,3},{6,4},{7,5},{8,6},{9,7},{10,... | collective-permute-start | bytes 196616 | tf_op jit(solution)/shard_map/ppermute | solution.py:9
  265.0 12.4 %collective-permute-start.3 = (f32[1,128,128]{2,1,0:T(8,128)S(1)}, f32[1,128,128]{2,1,0:T(8,128)S(1)}, u32[]{:S(2)}, u32[]{:S(2)}) collective-permute-start(f32[1,128,128]{2,1,0:T(8,128)S(1)} %get-tuple-element.18), channel_id=1, source_target_pairs={{0,2},{1,3},{2,4},{3,5},{4,6},{5,7},{6,8},{7,9},{8,10},{9,11},{10,... | collective-permute-start | bytes 196616 | tf_op jit(solution)/shard_map/ppermute | solution.py:9
  268.3 12.6 %collective-permute-start.4 = (f32[1,128,128]{2,1,0:T(8,128)S(1)}, f32[1,128,128]{2,1,0:T(8,128)S(1)}, u32[]{:S(2)}, u32[]{:S(2)}) collective-permute-start(f32[1,128,128]{2,1,0:T(8,128)S(1)} %get-tuple-element.17), channel_id=1, source_target_pairs={{0,29},{1,30},{2,31},{3,0},{4,1},{5,2},{6,3},{7,4},{8,5},{9,6},{10... | collective-permute-start | bytes 196616 | tf_op jit(solution)/shard_map/ppermute | solution.py:9
  271.4 9.6 %collective-permute-start.5 = (f32[1,128,128]{2,1,0:T(8,128)S(1)}, f32[1,128,128]{2,1,0:T(8,128)S(1)}, u32[]{:S(2)}, u32[]{:S(2)}) collective-permute-start(f32[1,128,128]{2,1,0:T(8,128)S(1)} %get-tuple-element.16), channel_id=1, source_target_pairs={{0,3},{1,4},{2,5},{3,6},{4,7},{5,8},{6,9},{7,10},{8,11},{9,12},{10... | collective-permute-start | bytes 196616 | tf_op jit(solution)/shard_map/ppermute | solution.py:9
  271.4 13.4 %collective-permute-start.6 = (f32[1,128,128]{2,1,0:T(8,128)S(1)}, f32[1,128,128]{2,1,0:T(8,128)S(1)}, u32[]{:S(2)}, u32[]{:S(2)}) collective-permute-start(f32[1,128,128]{2,1,0:T(8,128)S(1)} %get-tuple-element.15), channel_id=1, source_target_pairs={{0,28},{1,29},{2,30},{3,31},{4,0},{5,1},{6,2},{7,3},{8,4},{9,5},{1... | collective-permute-start | bytes 196616 | tf_op jit(solution)/shard_map/ppermute | solution.py:9
  277.3 9.3 %collective-permute-start.7 = (f32[1,128,128]{2,1,0:T(8,128)S(1)}, f32[1,128,128]{2,1,0:T(8,128)S(1)}, u32[]{:S(2)}, u32[]{:S(2)}) collective-permute-start(f32[1,128,128]{2,1,0:T(8,128)S(1)} %get-tuple-element.14), channel_id=1, source_target_pairs={{0,4},{1,5},{2,6},{3,7},{4,8},{5,9},{6,10},{7,11},{8,12},{9,13},{1... | collective-permute-start | bytes 196616 | tf_op jit(solution)/shard_map/ppermute | solution.py:9
  277.4 20.0 %collective-permute-start.8 = (f32[1,128,128]{2,1,0:T(8,128)S(1)}, f32[1,128,128]{2,1,0:T(8,128)S(1)}, u32[]{:S(2)}, u32[]{:S(2)}) collective-permute-start(f32[1,128,128]{2,1,0:T(8,128)S(1)} %get-tuple-element.13), channel_id=1, source_target_pairs={{0,27},{1,28},{2,29},{3,30},{4,31},{5,0},{6,1},{7,2},{8,3},{9,4},{... | collective-permute-start | bytes 196616 | tf_op jit(solution)/shard_map/ppermute | solution.py:9
  280.9 16.7 %collective-permute-start.9 = (f32[1,128,128]{2,1,0:T(8,128)S(1)}, f32[1,128,128]{2,1,0:T(8,128)S(1)}, u32[]{:S(2)}, u32[]{:S(2)}) collective-permute-start(f32[1,128,128]{2,1,0:T(8,128)S(1)} %get-tuple-element.12), channel_id=1, source_target_pairs={{0,5},{1,6},{2,7},{3,8},{4,9},{5,10},{6,11},{7,12},{8,13},{9,14},{... | collective-permute-start | bytes 196616 | tf_op jit(solution)/shard_map/ppermute | solution.py:9
  281.1 19.5 %collective-permute-start.10 = (f32[1,128,128]{2,1,0:T(8,128)S(1)}, f32[1,128,128]{2,1,0:T(8,128)S(1)}, u32[]{:S(2)}, u32[]{:S(2)}) collective-permute-start(f32[1,128,128]{2,1,0:T(8,128)S(1)} %get-tuple-element.11), channel_id=1, source_target_pairs={{0,26},{1,27},{2,28},{3,29},{4,30},{5,31},{6,0},{7,1},{8,2},{9,3},... | collective-permute-start | bytes 196616 | tf_op jit(solution)/shard_map/ppermute | solution.py:9
  284.8 15.7 %collective-permute-start.11 = (f32[1,128,128]{2,1,0:T(8,128)S(1)}, f32[1,128,128]{2,1,0:T(8,128)S(1)}, u32[]{:S(2)}, u32[]{:S(2)}) collective-permute-start(f32[1,128,128]{2,1,0:T(8,128)S(1)} %get-tuple-element.10), channel_id=1, source_target_pairs={{0,6},{1,7},{2,8},{3,9},{4,10},{5,11},{6,12},{7,13},{8,14},{9,15},... | collective-permute-start | bytes 196616 | tf_op jit(solution)/shard_map/ppermute | solution.py:9
  286.6 14.0 %collective-permute-start.12 = (f32[1,128,128]{2,1,0:T(8,128)S(1)}, f32[1,128,128]{2,1,0:T(8,128)S(1)}, u32[]{:S(2)}, u32[]{:S(2)}) collective-permute-start(f32[1,128,128]{2,1,0:T(8,128)S(1)} %get-tuple-element.9), channel_id=1, source_target_pairs={{0,25},{1,26},{2,27},{3,28},{4,29},{5,30},{6,31},{7,0},{8,1},{9,2}... | collective-permute-start | bytes 196616 | tf_op jit(solution)/shard_map/ppermute | solution.py:9
  297.4 8.7 %collective-permute-start.13 = (f32[1,128,128]{2,1,0:T(8,128)S(1)}, f32[1,128,128]{2,1,0:T(8,128)S(1)}, u32[]{:S(2)}, u32[]{:S(2)}) collective-permute-start(f32[1,128,128]{2,1,0:T(8,128)S(1)} %get-tuple-element.8), channel_id=1, source_target_pairs={{0,7},{1,8},{2,9},{3,10},{4,11},{5,12},{6,13},{7,14},{8,15},{9,16}... | collective-permute-start | bytes 196616 | tf_op jit(solution)/shard_map/ppermute | solution.py:9
  297.6 8.6 %collective-permute-start.14 = (f32[1,128,128]{2,1,0:T(8,128)S(1)}, f32[1,128,128]{2,1,0:T(8,128)S(1)}, u32[]{:S(2)}, u32[]{:S(2)}) collective-permute-start(f32[1,128,128]{2,1,0:T(8,128)S(1)} %get-tuple-element.7), channel_id=1, source_target_pairs={{0,16},{1,17},{2,18},{3,19},{4,20},{5,21},{6,22},{7,23},{8,24},{9,... | collective-permute-start | bytes 196616 | tf_op jit(solution)/shard_map/ppermute | solution.py:9
  306.1 1.0 copy-start.1
Sparse Core Ops, SparseCore 0:
  9.2 37.0 all-gather.6
  48.9 137.2 all-gather.4
  205.9 35.0 all-gather.8
where the time goes:
time: 314 us
  waiting for transfers between devices  202 us (64%)
  local copies, waits for them, and re-layouts  41.5 us (13%)
  starting transfers between devices  38.9 us (12%)
  matrix products  17.2 us (5%)
  between operations  13.4 us (4%)
    all_gather x1, waiting for transfers between devices, per_device(): gathered = lax.all_gather(density, 'col', axis=0, tiled=True)  128 us
    ppermute x15, starting transfers between devices, shifted(): lax.ppermute(value, axis, [(i, (i + by) % length) for i in range(length)])  38.8 us
    all_gather x1, waiting for transfers between devices, per_device(): column_blocks = lax.all_gather(density, 'row', axis=0, tiled=True)  33.8 us
    all_gather x1, waiting for transfers between devices, per_device(): square_panel = lax.all_gather(square_half[None], 'row', axis=0, tiled=True)  33 us
    gather x3, local copies, waits for them, and re-layouts, per_device(): from_square = square_panel[inner_row, mirror[found_slot], inner_local]  14.2 us
    gather x1, local copies, waits for them, and re-layouts, per_device(): right_blocks = column_blocks[target_rank[:, :, None], found_slot]  12.1 us
    gather x1, local copies, waits for them, and re-layouts, per_device(): left_blocks = gathered[source_col[:, None] * rows_here + local_ids[None, :]]  10.6 us
    dot_general x1, matrix products, per_device(): jnp.einsum('sltab,sltcb->slac', left_blocks, right_blocks, preferred_elem...  8.99 us
  transfers between devices with their start and end apart: 18, of which 4 were waited for; matrix products, arithmetic and copies ran while one was open for 6% of the time, Pallas kernels for 0%

commit v1 on v0

--- a/solution.py
+++ b/solution.py
@@ -1,7 +1,35 @@
+import functools
 import jax
 import jax.numpy as jnp
 from jax import lax
 from jax.sharding import PartitionSpec as P
+
+
+def trace_links(field, axis_name):
+    oldest = lax.axis_size(axis_name)
+    copies = []
+    g_now, then, newest = (oldest, lax.axis_index(axis_name), field.shape[0])
+    for dev_i in range(g_now):
+        copies.append((dev_i, (dev_i + 1) % g_now))
+    found = []
+    for dev_i in range(g_now):
+        found.append((dev_i, (dev_i - 1) % g_now))
+    new = jnp.zeros((*field.shape[:0], g_now * newest, *field.shape[1:]), field.dtype)
+    new = lax.dynamic_update_slice_in_dim(new, field, then * newest, axis=0)
+    front = vec_out = field
+    tall = g_now // 2
+    for at in range(1, tall + 1):
+        front = lax.ppermute(front, perm=copies, axis_name=axis_name)
+        new = lax.dynamic_update_slice_in_dim(new, front, (then - at) % g_now * newest, axis=0)
+        if at < g_now - tall:
+            vec_out = lax.ppermute(vec_out, perm=found, axis_name=axis_name)
+            new = lax.dynamic_update_slice_in_dim(
+                new, vec_out, (then + at) % g_now * newest, axis=0
+            )
+    return new
+
+
+define_keys_up = functools.partial(trace_links, axis_name="row")
 
 
 def shifted(value, axis, by):
@@ -46,7 +74,7 @@
     present_mask = present[..., None, None]
     gathered = lax.all_gather(density, "col", axis=0, tiled=True)
     left_blocks = gathered[source_col[:, None] * rows_here + local_ids[None, :]]
-    column_blocks = lax.all_gather(density, "row", axis=0, tiled=True)
+    column_blocks = define_keys_up(density)
     right_blocks = column_blocks[target_rank[:, :, None], found_slot]
     right_blocks = jnp.where(present_mask, right_blocks, jnp.zeros((), right_blocks.dtype))
     square_tile = jnp.einsum(

time: 314 us -> 278 us (0.89)
  waiting for transfers between devices: 202 us -> 145 us
  local copies, waits for them, and re-layouts: 41.5 us -> 52.6 us
  starting transfers between devices: 38.9 us -> 47.8 us
    all_gather x1, waiting for transfers between devices: 128 us -> 89.7 us  [per_device(): gathered = lax.all_gather(density, 'col', axis=0, tiled=True)]
    all_gather x1 -> x0, waiting for transfers between devices: 33.8 us -> none  [per_device(): column_blocks = lax.all_gather(density, 'row', axis=0, tiled=True)]
    ppermute x0 -> x7, waiting for transfers between devices: none -> 16.3 us  [the longest x4 14.4 us: trace_links(): front = lax.ppermute(front, perm=copies, axis_name=axis_name)]
    ppermute x0 -> x7, starting transfers between devices: none -> 8.87 us  [the longest x3 8.84 us: trace_links(): vec_out = lax.ppermute(vec_out, perm=found, axis_name=axis_name)]
    dynamic_update_slice x0 -> x8, local copies, waits for them, and re-layouts: none -> 7.77 us  [the longest x4 3.37 us: trace_links(): lax.dynamic_update_slice_in_dim(new, front, (then - at) % g_now * newest,...]
  transfers between devices with their start and end apart: 18 -> 24, of which waited for: 4 -> 8; matrix products, arithmetic and copies ran while one was open for 6% -> 11% of each run, Pallas kernels for 0% -> 0%
where the time goes in v1:
time: 278 us
  waiting for transfers between devices  145 us (52%)
  local copies, waits for them, and re-layouts  52.6 us (19%)
  starting transfers between devices  47.8 us (17%)
  matrix products  17.2 us (6%)
  between operations  13.7 us (5%)
    all_gather x1, waiting for transfers between devices, per_device(): gathered = lax.all_gather(density, 'col', axis=0, tiled=True)  89.7 us
    ppermute x15, starting transfers between devices, shifted(): lax.ppermute(value, axis, [(i, (i + by) % length) for i in range(length)])  38.8 us
    all_gather x1, waiting for transfers between devices, per_device(): square_panel = lax.all_gather(square_half[None], 'row', axis=0, tiled=True)  33 us
    ppermute x4, waiting for transfers between devices, trace_links(): front = lax.ppermute(front, perm=copies, axis_name=axis_name)  14.4 us
    gather x3, local copies, waits for them, and re-layouts, per_device(): from_square = square_panel[inner_row, mirror[found_slot], inner_local]  14.2 us
    gather x1, local copies, waits for them, and re-layouts, per_device(): right_blocks = column_blocks[target_rank[:, :, None], found_slot]  12.3 us
    gather x1, local copies, waits for them, and re-layouts, per_device(): left_blocks = gathered[source_col[:, None] * rows_here + local_ids[None, :]]  10.6 us
    dot_general x1, matrix products, per_device(): jnp.einsum('sltab,sltcb->slac', left_blocks, right_blocks, preferred_elem...  9 us
  transfers between devices with their start and end apart: 24, of which 8 were waited for; matrix products, arithmetic and copies ran while one was open for 11% of the time, Pallas kernels for 0%

profile of v1, /device:TPU:48, one launch (start us, length us, event | category | flops | bytes accessed | tf_op | source)
XLA Modules:
  0.0 278.1 jit_solution(16338076315306530872)
XLA Ops:
  6.5 0.7 all-gather.4.cloned.1.call-update
  7.3 0.0 all-gather.6.cloned.1.call-start
  7.3 0.0 collective-permute-start
  7.3 2.9 %collective-permute-start.1 = (bf16[1,16,128,128]{3,2,1,0:T(8,128)(2,1)}, bf16[1,16,128,128]{3,2,1,0:T(8,128)(2,1)S(1)}, u32[]{:S(2)}, u32[]{:S(2)}) collective-permute-start(bf16[1,16,128,128]{3,2,1,0:T(8,128)(2,1)} %param.4), channel_id=1, source_target_pairs={{0,224},{32,0},{64,32},{96,64},{128,96},{160,128},{192,160},{224,1... | collective-permute-start | bytes 1572872 | tf_op jit(solution)/shard_map/ppermute | solution.py:25
  10.3 0.8 copy.11
  11.1 0.7 compare_select_fusion.6
  11.8 0.6 gather_fusion.1
  12.4 0.7 gather_fusion.2
  13.1 0.6 gather_fusion.3
  13.6 0.4 fusion.19
  14.1 3.3 %collective-permute-done = bf16[1,16,128,128]{3,2,1,0:T(8,128)(2,1)S(1)} collective-permute-done((bf16[1,16,128,128]{3,2,1,0:T(8,128)(2,1)}, bf16[1,16,128,128]{3,2,1,0:T(8,128)(2,1)S(1)}, u32[]{:S(2)}, u32[]{:S(2)}) %collective-permute-start) | collective-permute-done | bytes 524320 | tf_op jit(solution)/shard_map/ppermute | solution.py:22
  17.4 0.1 broadcast_in_dim.61
  17.5 3.0 %collective-permute-start.3 = (bf16[1,16,128,128]{3,2,1,0:T(8,128)(2,1)S(1)}, bf16[1,16,128,128]{3,2,1,0:T(8,128)(2,1)S(1)}, u32[]{:S(2)}, u32[]{:S(2)}) collective-permute-start(bf16[1,16,128,128]{3,2,1,0:T(8,128)(2,1)S(1)} %collective-permute-done.1), channel_id=1, source_target_pairs={{0,224},{32,0},{64,32},{96,64},{128,96},{160,128},{192,160},{224,1... | collective-permute-start | bytes 1572872 | tf_op jit(solution)/shard_map/ppermute | solution.py:25
  20.4 6.7 %collective-permute-done.2 = bf16[1,16,128,128]{3,2,1,0:T(8,128)(2,1)S(1)} collective-permute-done((bf16[1,16,128,128]{3,2,1,0:T(8,128)(2,1)S(1)}, bf16[1,16,128,128]{3,2,1,0:T(8,128)(2,1)S(1)}, u32[]{:S(2)}, u32[]{:S(2)}) %collective-permute-start.2) | collective-permute-done | bytes 524320 | tf_op jit(solution)/shard_map/ppermute | solution.py:22
  27.2 0.0 collective-permute-start.4
  27.2 0.1 reshape.430
  27.3 0.4 compare_reduce_fusion
  27.7 3.0 %broadcast_in_dim.60 = bf16[8,16,128,128]{3,2,1,0:T(8,128)(2,1)} broadcast(bf16[]{:T(256)} %constant.149.clone.1), dimensions={} | broadcast | bytes 4194306 | tf_op jit(solution)/shard_map/broadcast_in_dim | solution.py:17
  30.7 1.9 constant_dynamic-update-slice_fusion.7
  32.6 0.0 collective-permute-done.3
  32.6 2.9 %collective-permute-start.5 = (bf16[1,16,128,128]{3,2,1,0:T(8,128)(2,1)S(1)}, bf16[1,16,128,128]{3,2,1,0:T(8,128)(2,1)S(1)}, u32[]{:S(2)}, u32[]{:S(2)}) collective-permute-start(bf16[1,16,128,128]{3,2,1,0:T(8,128)(2,1)S(1)} %collective-permute-done.3), channel_id=1, source_target_pairs={{0,224},{32,0},{64,32},{96,64},{128,96},{160,128},{192,160},{224,1... | collective-permute-start | bytes 1572872 | tf_op jit(solution)/shard_map/ppermute | solution.py:25
  35.5 0.8 constant_dynamic-update-slice_fusion.6
  36.3 0.6 collective-permute-done.4
  37.0 0.9 constant_dynamic-update-slice_fusion.5
  37.8 0.8 constant_dynamic-update-slice_fusion.4
  38.7 0.8 constant_dynamic-update-slice_fusion.3
  39.5 0.8 constant_dynamic-update-slice_fusion.2
  40.4 1.9 collective-permute-done.5
  42.2 0.8 constant_dynamic-update-slice_fusion.1
  43.0 3.8 %collective-permute-done.6 = bf16[1,16,128,128]{3,2,1,0:T(8,128)(2,1)S(1)} collective-permute-done((bf16[1,16,128,128]{3,2,1,0:T(8,128)(2,1)S(1)}, bf16[1,16,128,128]{3,2,1,0:T(8,128)(2,1)S(1)}, u32[]{:S(2)}, u32[]{:S(2)}) %collective-permute-start.6) | collective-permute-done | bytes 524320 | tf_op jit(solution)/shard_map/ppermute | solution.py:22
  46.8 0.9 constant_dynamic-update-slice_fusion
  47.6 12.3 %gather_fusion.4 = bf16[256,128,128]{2,1,0:T(8,128)(2,1)} fusion(bf16[8,16,128,128]{3,2,1,0:T(8,128)(2,1)} %constant_dynamic-update-slice_fusion, s32[256]{0:T(256)S(1)} %reshape.430), kind=kCustom, calls=%fused_computation.4 | custom fusion | bytes 16779264 | tf_op jit(solution)/shard_map/gather | solution.py:78
  60.0 89.7 %all-gather.4.cloned.1.call-done = bf16[32,16,128,128]{3,2,1,0:T(8,128)(2,1)} async-done(((bf16[1,16,128,128]{3,2,1,0:T(8,128)(2,1)}), bf16[32,16,128,128]{3,2,1,0:T(8,128)(2,1)}) %all-gather.4.cloned.1.call-update) | async-done | bytes 16777232 | tf_op jit(solution)/shard_map/all_gather | solution.py:75
  149.7 10.6 %gather_fusion = bf16[16,16,128,128]{3,2,1,0:T(8,128)(2,1)} fusion(bf16[32,16,128,128]{3,2,1,0:T(8,128)(2,1)} %all-gather.4.cloned.1.call-done, s32[1024]{0:T(1024)S(1)} %pad_clamp_fusion.3), kind=kCustom, calls=%fused_computation | custom fusion | bytes 16777280 | tf_op jit(solution)/shard_map/gather | solution.py:76
  160.3 9.0 %fusion.37 = (bf16[16,128,128]{2,1,0:T(8,128)(2,1)}, f32[16,128,128]{2,1,0:T(8,128)S(1)}) fusion(bf16[16,16,128,128]{3,2,1,0:T(8,128)(2,1)} %gather_fusion, bf16[16,16,128,128]{3,2,1,0:T(8,128)(2,1)} %bitcast.90, pred[16,16]{1,0:T(8,128)(4,1)S(1)} %compare_reduce_fusion), kind=kOutput, calls=%fused_computation.96 | convolution fusion | flops 1078198272 | bytes 18350336 | tf_op jit(solution)/shard_map/sltab,sltcb->slac/dot_general | solution.py:80
  169.3 0.0 all-gather.6.cloned.1.call-update
  169.3 0.1 reshape.438
  169.4 1.9 gather_fusion.5
  171.3 0.1 gather.43
  171.4 0.1 reshape.446
  171.5 33.0 %all-gather.6.cloned.1.call-done = bf16[128,128,128]{2,1,0:T(8,128)(2,1)} async-done(((bf16[16,128,128]{2,1,0:T(8,128)(2,1)}), bf16[128,128,128]{2,1,0:T(8,128)(2,1)}) %all-gather.6.cloned.1.call-update) | async-done | bytes 4194320 | tf_op jit(solution)/shard_map/all_gather | solution.py:84
  204.5 12.3 %gather_fusion.6 = bf16[256,128,128]{2,1,0:T(8,128)(2,1)} fusion(bf16[8,16,1,128,128]{4,3,1,0,2:T(8,128)(2,1)} %bitcast.89, s32[256]{0:T(256)S(1)} %reshape.446), kind=kCustom, calls=%fused_computation.6 | custom fusion | bytes 16780288 | tf_op jit(solution)/shard_map/gather | solution.py:87
  216.8 8.2 %multiply_subtract_fusion = f32[16,128,128]{2,1,0:T(8,128)S(1)} fusion(f32[16,128,128]{2,1,0:T(8,128)S(1)} %get-tuple-element.23, bf16[16,16,128,128]{3,2,1,0:T(8,128)(2,1)} %gather_fusion, bf16[16,16,128,128]{3,2,1,0:T(8,128)(2,1)} %bitcast.91, pred[16,16]{1,0:T(8,128)(4,1)S(1)} %compare_reduce_fusion), kind=kOutput, calls=%fused_computation.18 | convolution fusion | flops 1078722560 | bytes 18874624 | tf_op jit(solution)/shard_map/sltab,sltbc->slac/dot_general | solution.py:89
  225.0 0.1 fusion.36
  225.1 0.8 collective-permute-start.7
  225.9 1.5 collective-permute-start.8
  227.4 1.2 collective-permute-start.9
  228.6 3.3 %collective-permute-start.10 = (f32[1,128,128]{2,1,0:T(8,128)S(1)}, f32[1,128,128]{2,1,0:T(8,128)S(1)}, u32[]{:S(2)}, u32[]{:S(2)}) collective-permute-start(f32[1,128,128]{2,1,0:T(8,128)S(1)} %get-tuple-element.18), channel_id=1, source_target_pairs={{0,2},{1,3},{2,4},{3,5},{4,6},{5,7},{6,8},{7,9},{8,10},{9,11},{10,... | collective-permute-start | bytes 196616 | tf_op jit(solution)/shard_map/ppermute | solution.py:37
  231.8 3.2 %collective-permute-start.11 = (f32[1,128,128]{2,1,0:T(8,128)S(1)}, f32[1,128,128]{2,1,0:T(8,128)S(1)}, u32[]{:S(2)}, u32[]{:S(2)}) collective-permute-start(f32[1,128,128]{2,1,0:T(8,128)S(1)} %get-tuple-element.17), channel_id=1, source_target_pairs={{0,29},{1,30},{2,31},{3,0},{4,1},{5,2},{6,3},{7,4},{8,5},{9,6},{10... | collective-permute-start | bytes 196616 | tf_op jit(solution)/shard_map/ppermute | solution.py:37
  235.0 5.9 %collective-permute-start.13 = (f32[1,128,128]{2,1,0:T(8,128)S(1)}, f32[1,128,128]{2,1,0:T(8,128)S(1)}, u32[]{:S(2)}, u32[]{:S(2)}) collective-permute-start(f32[1,128,128]{2,1,0:T(8,128)S(1)} %get-tuple-element.15), channel_id=1, source_target_pairs={{0,28},{1,29},{2,30},{3,31},{4,0},{5,1},{6,2},{7,3},{8,4},{9,5},{1... | collective-permute-start | bytes 196616 | tf_op jit(solution)/shard_map/ppermute | solution.py:37
  240.9 0.1 collective-permute-start.14
  241.0 0.0 collective-permute-done.10
  241.0 3.4 %collective-permute-start.15 = (f32[1,128,128]{2,1,0:T(8,128)S(1)}, f32[1,128,128]{2,1,0:T(8,128)S(1)}, u32[]{:S(2)}, u32[]{:S(2)}) collective-permute-start(f32[1,128,128]{2,1,0:T(8,128)S(1)} %get-tuple-element.13), channel_id=1, source_target_pairs={{0,27},{1,28},{2,29},{3,30},{4,31},{5,0},{6,1},{7,2},{8,3},{9,4},{... | collective-permute-start | bytes 196616 | tf_op jit(solution)/shard_map/ppermute | solution.py:37
  244.5 0.0 collective-permute-done.11
  244.5 0.2 collective-permute-start.16
  244.6 0.0 collective-permute-done.12
  244.6 3.7 %collective-permute-start.17 = (f32[1,128,128]{2,1,0:T(8,128)S(1)}, f32[1,128,128]{2,1,0:T(8,128)S(1)}, u32[]{:S(2)}, u32[]{:S(2)}) collective-permute-start(f32[1,128,128]{2,1,0:T(8,128)S(1)} %get-tuple-element.11), channel_id=1, source_target_pairs={{0,26},{1,27},{2,28},{3,29},{4,30},{5,31},{6,0},{7,1},{8,2},{9,3},... | collective-permute-start | bytes 196616 | tf_op jit(solution)/shard_map/ppermute | solution.py:37
  248.4 1.7 collective-permute-start.18
  250.2 10.8 %collective-permute-start.19 = (f32[1,128,128]{2,1,0:T(8,128)S(1)}, f32[1,128,128]{2,1,0:T(8,128)S(1)}, u32[]{:S(2)}, u32[]{:S(2)}) collective-permute-start(f32[1,128,128]{2,1,0:T(8,128)S(1)} %get-tuple-element.9), channel_id=1, source_target_pairs={{0,25},{1,26},{2,27},{3,28},{4,29},{5,30},{6,31},{7,0},{8,1},{9,2}... | collective-permute-start | bytes 196616 | tf_op jit(solution)/shard_map/ppermute | solution.py:37
  261.0 0.1 collective-permute-start.20
  261.1 3.0 %collective-permute-start.21 = (f32[1,128,128]{2,1,0:T(8,128)S(1)}, f32[1,128,128]{2,1,0:T(8,128)S(1)}, u32[]{:S(2)}, u32[]{:S(2)}) collective-permute-start(f32[1,128,128]{2,1,0:T(8,128)S(1)} %get-tuple-element.7), channel_id=1, source_target_pairs={{0,16},{1,17},{2,18},{3,19},{4,20},{5,21},{6,22},{7,23},{8,24},{9,... | collective-permute-start | bytes 196616 | tf_op jit(solution)/shard_map/ppermute | solution.py:37
  264.2 5.5 %collective-permute-done.20 = f32[1,128,128]{2,1,0:T(8,128)S(1)} collective-permute-done((f32[1,128,128]{2,1,0:T(8,128)S(1)}, f32[1,128,128]{2,1,0:T(8,128)S(1)}, u32[]{:S(2)}, u32[]{:S(2)}) %collective-permute-start.20) | collective-permute-done | bytes 65568 | tf_op jit(solution)/shard_map/ppermute | solution.py:37
  269.7 1.0 copy-done.1
  270.7 0.6 bitcast_dynamic-update-slice_fusion
  (52 shorter events, 0.3 us)
Async XLA Ops:
  6.5 143.2 %all-gather.4.cloned.1.call-start = ((), (), s32[]{:S(2)}) async-start(), calls=%async_computation | async-start | bytes 17301504 | tf_op jit(solution)/shard_map/all_gather | solution.py:75
  7.3 197.2 %all-gather.6.cloned.1.call-start = ((), (), s32[]{:S(2)}) async-start(), calls=%async_computation.1 | async-start | bytes 4718592 | tf_op jit(solution)/shard_map/all_gather | solution.py:84
  7.3 10.0 %collective-permute-start = (bf16[1,16,128,128]{3,2,1,0:T(8,128)(2,1)}, bf16[1,16,128,128]{3,2,1,0:T(8,128)(2,1)S(1)}, u32[]{:S(2)}, u32[]{:S(2)}) collective-permute-start(bf16[1,16,128,128]{3,2,1,0:T(8,128)(2,1)} %param.4), channel_id=1, source_target_pairs={{0,32},{32,64},{64,96},{96,128},{128,160},{160,192},{192,224},{224... | collective-permute-start | bytes 1572872 | tf_op jit(solution)/shard_map/ppermute | solution.py:22
  7.3 10.1 %collective-permute-start.1 = (bf16[1,16,128,128]{3,2,1,0:T(8,128)(2,1)}, bf16[1,16,128,128]{3,2,1,0:T(8,128)(2,1)S(1)}, u32[]{:S(2)}, u32[]{:S(2)}) collective-permute-start(bf16[1,16,128,128]{3,2,1,0:T(8,128)(2,1)} %param.4), channel_id=1, source_target_pairs={{0,224},{32,0},{64,32},{96,64},{128,96},{160,128},{192,160},{224,1... | collective-permute-start | bytes 1572872 | tf_op jit(solution)/shard_map/ppermute | solution.py:25
  17.3 9.8 %collective-permute-start.2 = (bf16[1,16,128,128]{3,2,1,0:T(8,128)(2,1)S(1)}, bf16[1,16,128,128]{3,2,1,0:T(8,128)(2,1)S(1)}, u32[]{:S(2)}, u32[]{:S(2)}) collective-permute-start(bf16[1,16,128,128]{3,2,1,0:T(8,128)(2,1)S(1)} %collective-permute-done), channel_id=1, source_target_pairs={{0,32},{32,64},{64,96},{96,128},{128,160},{160,192},{192,224},{224... | collective-permute-start | bytes 1572872 | tf_op jit(solution)/shard_map/ppermute | solution.py:22
  17.5 15.1 %collective-permute-start.3 = (bf16[1,16,128,128]{3,2,1,0:T(8,128)(2,1)S(1)}, bf16[1,16,128,128]{3,2,1,0:T(8,128)(2,1)S(1)}, u32[]{:S(2)}, u32[]{:S(2)}) collective-permute-start(bf16[1,16,128,128]{3,2,1,0:T(8,128)(2,1)S(1)} %collective-permute-done.1), channel_id=1, source_target_pairs={{0,224},{32,0},{64,32},{96,64},{128,96},{160,128},{192,160},{224,1... | collective-permute-start | bytes 1572872 | tf_op jit(solution)/shard_map/ppermute | solution.py:25
  27.2 9.8 %collective-permute-start.4 = (bf16[1,16,128,128]{3,2,1,0:T(8,128)(2,1)S(1)}, bf16[1,16,128,128]{3,2,1,0:T(8,128)(2,1)S(1)}, u32[]{:S(2)}, u32[]{:S(2)}) collective-permute-start(bf16[1,16,128,128]{3,2,1,0:T(8,128)(2,1)S(1)} %collective-permute-done.2), channel_id=1, source_target_pairs={{0,32},{32,64},{64,96},{96,128},{128,160},{160,192},{192,224},{224... | collective-permute-start | bytes 1572872 | tf_op jit(solution)/shard_map/ppermute | solution.py:22
  32.6 9.6 %collective-permute-start.5 = (bf16[1,16,128,128]{3,2,1,0:T(8,128)(2,1)S(1)}, bf16[1,16,128,128]{3,2,1,0:T(8,128)(2,1)S(1)}, u32[]{:S(2)}, u32[]{:S(2)}) collective-permute-start(bf16[1,16,128,128]{3,2,1,0:T(8,128)(2,1)S(1)} %collective-permute-done.3), channel_id=1, source_target_pairs={{0,224},{32,0},{64,32},{96,64},{128,96},{160,128},{192,160},{224,1... | collective-permute-start | bytes 1572872 | tf_op jit(solution)/shard_map/ppermute | solution.py:25
  37.0 9.8 %collective-permute-start.6 = (bf16[1,16,128,128]{3,2,1,0:T(8,128)(2,1)S(1)}, bf16[1,16,128,128]{3,2,1,0:T(8,128)(2,1)S(1)}, u32[]{:S(2)}, u32[]{:S(2)}) collective-permute-start(bf16[1,16,128,128]{3,2,1,0:T(8,128)(2,1)S(1)} %collective-permute-done.4), channel_id=1, source_target_pairs={{0,32},{32,64},{64,96},{96,128},{128,160},{160,192},{192,224},{224... | collective-permute-start | bytes 1572872 | tf_op jit(solution)/shard_map/ppermute | solution.py:22
  160.3 9.1 %copy-start = (s32[16]{0:T(128)S(1)}, s32[16]{0:T(128)}, u32[]{:S(2)}) copy-start(s32[16]{0:T(128)} %constant.163.clone) | copy-start | bytes 196
  225.1 9.9 %collective-permute-start.7 = (f32[1,128,128]{2,1,0:T(8,128)S(1)}, f32[1,128,128]{2,1,0:T(8,128)S(1)}, u32[]{:S(2)}, u32[]{:S(2)}) collective-permute-start(f32[1,128,128]{2,1,0:T(8,128)S(1)} %get-tuple-element.21), channel_id=1, source_target_pairs={{0,31},{1,0},{2,1},{3,2},{4,3},{5,4},{6,5},{7,6},{8,7},{9,8},{10,9... | collective-permute-start | bytes 196616 | tf_op jit(solution)/shard_map/ppermute | solution.py:37
  225.9 9.1 %collective-permute-start.8 = (f32[1,128,128]{2,1,0:T(8,128)S(1)}, f32[1,128,128]{2,1,0:T(8,128)S(1)}, u32[]{:S(2)}, u32[]{:S(2)}) collective-permute-start(f32[1,128,128]{2,1,0:T(8,128)S(1)} %get-tuple-element.20), channel_id=1, source_target_pairs={{0,1},{1,2},{2,3},{3,4},{4,5},{5,6},{6,7},{7,8},{8,9},{9,10},{10,1... | collective-permute-start | bytes 196616 | tf_op jit(solution)/shard_map/ppermute | solution.py:37
  227.4 13.5 %collective-permute-start.9 = (f32[1,128,128]{2,1,0:T(8,128)S(1)}, f32[1,128,128]{2,1,0:T(8,128)S(1)}, u32[]{:S(2)}, u32[]{:S(2)}) collective-permute-start(f32[1,128,128]{2,1,0:T(8,128)S(1)} %get-tuple-element.19), channel_id=1, source_target_pairs={{0,30},{1,31},{2,0},{3,1},{4,2},{5,3},{6,4},{7,5},{8,6},{9,7},{10,... | collective-permute-start | bytes 196616 | tf_op jit(solution)/shard_map/ppermute | solution.py:37
  228.6 12.4 %collective-permute-start.10 = (f32[1,128,128]{2,1,0:T(8,128)S(1)}, f32[1,128,128]{2,1,0:T(8,128)S(1)}, u32[]{:S(2)}, u32[]{:S(2)}) collective-permute-start(f32[1,128,128]{2,1,0:T(8,128)S(1)} %get-tuple-element.18), channel_id=1, source_target_pairs={{0,2},{1,3},{2,4},{3,5},{4,6},{5,7},{6,8},{7,9},{8,10},{9,11},{10,... | collective-permute-start | bytes 196616 | tf_op jit(solution)/shard_map/ppermute | solution.py:37
  231.8 12.6 %collective-permute-start.11 = (f32[1,128,128]{2,1,0:T(8,128)S(1)}, f32[1,128,128]{2,1,0:T(8,128)S(1)}, u32[]{:S(2)}, u32[]{:S(2)}) collective-permute-start(f32[1,128,128]{2,1,0:T(8,128)S(1)} %get-tuple-element.17), channel_id=1, source_target_pairs={{0,29},{1,30},{2,31},{3,0},{4,1},{5,2},{6,3},{7,4},{8,5},{9,6},{10... | collective-permute-start | bytes 196616 | tf_op jit(solution)/shard_map/ppermute | solution.py:37
  235.0 9.6 %collective-permute-start.12 = (f32[1,128,128]{2,1,0:T(8,128)S(1)}, f32[1,128,128]{2,1,0:T(8,128)S(1)}, u32[]{:S(2)}, u32[]{:S(2)}) collective-permute-start(f32[1,128,128]{2,1,0:T(8,128)S(1)} %get-tuple-element.16), channel_id=1, source_target_pairs={{0,3},{1,4},{2,5},{3,6},{4,7},{5,8},{6,9},{7,10},{8,11},{9,12},{10... | collective-permute-start | bytes 196616 | tf_op jit(solution)/shard_map/ppermute | solution.py:37
  235.0 13.4 %collective-permute-start.13 = (f32[1,128,128]{2,1,0:T(8,128)S(1)}, f32[1,128,128]{2,1,0:T(8,128)S(1)}, u32[]{:S(2)}, u32[]{:S(2)}) collective-permute-start(f32[1,128,128]{2,1,0:T(8,128)S(1)} %get-tuple-element.15), channel_id=1, source_target_pairs={{0,28},{1,29},{2,30},{3,31},{4,0},{5,1},{6,2},{7,3},{8,4},{9,5},{1... | collective-permute-start | bytes 196616 | tf_op jit(solution)/shard_map/ppermute | solution.py:37
  240.9 9.3 %collective-permute-start.14 = (f32[1,128,128]{2,1,0:T(8,128)S(1)}, f32[1,128,128]{2,1,0:T(8,128)S(1)}, u32[]{:S(2)}, u32[]{:S(2)}) collective-permute-start(f32[1,128,128]{2,1,0:T(8,128)S(1)} %get-tuple-element.14), channel_id=1, source_target_pairs={{0,4},{1,5},{2,6},{3,7},{4,8},{5,9},{6,10},{7,11},{8,12},{9,13},{1... | collective-permute-start | bytes 196616 | tf_op jit(solution)/shard_map/ppermute | solution.py:37
  241.0 20.0 %collective-permute-start.15 = (f32[1,128,128]{2,1,0:T(8,128)S(1)}, f32[1,128,128]{2,1,0:T(8,128)S(1)}, u32[]{:S(2)}, u32[]{:S(2)}) collective-permute-start(f32[1,128,128]{2,1,0:T(8,128)S(1)} %get-tuple-element.13), channel_id=1, source_target_pairs={{0,27},{1,28},{2,29},{3,30},{4,31},{5,0},{6,1},{7,2},{8,3},{9,4},{... | collective-permute-start | bytes 196616 | tf_op jit(solution)/shard_map/ppermute | solution.py:37
  244.5 16.6 %collective-permute-start.16 = (f32[1,128,128]{2,1,0:T(8,128)S(1)}, f32[1,128,128]{2,1,0:T(8,128)S(1)}, u32[]{:S(2)}, u32[]{:S(2)}) collective-permute-start(f32[1,128,128]{2,1,0:T(8,128)S(1)} %get-tuple-element.12), channel_id=1, source_target_pairs={{0,5},{1,6},{2,7},{3,8},{4,9},{5,10},{6,11},{7,12},{8,13},{9,14},{... | collective-permute-start | bytes 196616 | tf_op jit(solution)/shard_map/ppermute | solution.py:37
  244.6 19.5 %collective-permute-start.17 = (f32[1,128,128]{2,1,0:T(8,128)S(1)}, f32[1,128,128]{2,1,0:T(8,128)S(1)}, u32[]{:S(2)}, u32[]{:S(2)}) collective-permute-start(f32[1,128,128]{2,1,0:T(8,128)S(1)} %get-tuple-element.11), channel_id=1, source_target_pairs={{0,26},{1,27},{2,28},{3,29},{4,30},{5,31},{6,0},{7,1},{8,2},{9,3},... | collective-permute-start | bytes 196616 | tf_op jit(solution)/shard_map/ppermute | solution.py:37
  248.4 15.7 %collective-permute-start.18 = (f32[1,128,128]{2,1,0:T(8,128)S(1)}, f32[1,128,128]{2,1,0:T(8,128)S(1)}, u32[]{:S(2)}, u32[]{:S(2)}) collective-permute-start(f32[1,128,128]{2,1,0:T(8,128)S(1)} %get-tuple-element.10), channel_id=1, source_target_pairs={{0,6},{1,7},{2,8},{3,9},{4,10},{5,11},{6,12},{7,13},{8,14},{9,15},... | collective-permute-start | bytes 196616 | tf_op jit(solution)/shard_map/ppermute | solution.py:37
  250.2 14.0 %collective-permute-start.19 = (f32[1,128,128]{2,1,0:T(8,128)S(1)}, f32[1,128,128]{2,1,0:T(8,128)S(1)}, u32[]{:S(2)}, u32[]{:S(2)}) collective-permute-start(f32[1,128,128]{2,1,0:T(8,128)S(1)} %get-tuple-element.9), channel_id=1, source_target_pairs={{0,25},{1,26},{2,27},{3,28},{4,29},{5,30},{6,31},{7,0},{8,1},{9,2}... | collective-permute-start | bytes 196616 | tf_op jit(solution)/shard_map/ppermute | solution.py:37
  261.0 8.7 %collective-permute-start.20 = (f32[1,128,128]{2,1,0:T(8,128)S(1)}, f32[1,128,128]{2,1,0:T(8,128)S(1)}, u32[]{:S(2)}, u32[]{:S(2)}) collective-permute-start(f32[1,128,128]{2,1,0:T(8,128)S(1)} %get-tuple-element.8), channel_id=1, source_target_pairs={{0,7},{1,8},{2,9},{3,10},{4,11},{5,12},{6,13},{7,14},{8,15},{9,16}... | collective-permute-start | bytes 196616 | tf_op jit(solution)/shard_map/ppermute | solution.py:37
  261.1 8.6 %collective-permute-start.21 = (f32[1,128,128]{2,1,0:T(8,128)S(1)}, f32[1,128,128]{2,1,0:T(8,128)S(1)}, u32[]{:S(2)}, u32[]{:S(2)}) collective-permute-start(f32[1,128,128]{2,1,0:T(8,128)S(1)} %get-tuple-element.7), channel_id=1, source_target_pairs={{0,16},{1,17},{2,18},{3,19},{4,20},{5,21},{6,22},{7,23},{8,24},{9,... | collective-permute-start | bytes 196616 | tf_op jit(solution)/shard_map/ppermute | solution.py:37
  269.7 1.0 copy-start.1
Sparse Core Ops, SparseCore 0:
  9.9 139.7 all-gather.3
  169.4 35.0 all-gather.5
